TPU v7x, 128 devices: a whole 4x4x4 slice. The times are simulated.
128 devices in a mesh: blk: 32 (over x, z_hi, y), org: 4 (over z_lo, core).
Axes of the slice: x: 4, y: 4, z: 4 (z_hi: 2, z_lo: 2; z = z_hi * 2 + z_lo), core: 2. Of those that a mesh axis runs over, the one named last changes fastest.
Arguments:
- warm_labels: float32 [256, 512, 1024], P('blk', None, 'org'), may hold values from 0 to 6
- link_costs: float32 [4, 256, 512], P(None, 'blk'), may hold values from 0.05 to 1.5
- anchor_nodes: int32 [1024], P('org'), may hold values from 0 to 131071
- demand: float32 [1024], P('org'), may hold values from 0.2 to 2
Outputs:
- labels: float32 [256, 512, 1024], P('blk', None, 'org')
- link_weights: float32 [4, 256, 512], P(None, 'blk', 'org')
Inputs may be any that keep to these rules, and one draw needn't show every extreme that they name: `anchor_nodes`: node numbers r * 512 + c.
All inputs are finite; a program needn't handle non-finite values.
Results may differ from a plain program's by a relative error of at most 0.0003.
Values sent between devices are 32-bit elements; how exact they have to be, the bound alone decides.
No kernel may reach another device: no remote copies, remote signals or barrier semaphores. Data moves between devices by JAX's collectives and lax.ppermute only.
A program may use at most 128 MiB of HBM per device.

v0:
```python
import functools
import jax
import jax.numpy as jnp
from jax import lax
from jax.experimental import pallas as pl
from jax.experimental.pallas import tpu as pltpu
from jax.sharding import PartitionSpec as P


ANCHORS = 1024
STEPS = 6
EDGE = 6
FIRST = 3
SECOND = STEPS - 1 - FIRST
PAD = 8
CH = 128
far_value = 1000000000.0
temper = 0.5
F32 = jnp.float32
WEST, EAST, NORTH, SOUTH = range(4)
OUTER = (NORTH, SOUTH)
INNER_SIDE = (SOUTH, NORTH)


def row_of(side, depth):
    return depth if side == 0 else 7 - depth


def cost_row(side, depth):
    return EDGE + row_of(side, depth)


def chunks(cols, body):
    def step(i, carry):
        body(pl.multiple_of(i * CH, CH))
        return carry

    lax.fori_loop(0, cols // CH, step, 0)


def half_lanes(h):
    return pl.ds(h * 128, 128)


def clear_pads(buf, rows, cols):
    zero = jnp.zeros((PAD, 128), F32)
    for r in range(rows):
        for h in range(2):
            buf[r, h, pl.ds(0, PAD), :] = zero
            buf[r, h, pl.ds(cols + PAD, PAD), :] = zero


def anchored(values, anchors, node0):
    ids = node0 + lax.broadcasted_iota(jnp.int32, values.shape, 0)
    return jnp.where(ids == anchors, 0.0, values)


def add_lane_sum(sums, side, row, piece, terms):
    at = side * 8 + row
    sums[piece, at : at + 1, :] += jnp.sum(terms, axis=1)[None, :]


def lead_kernel(info, own, costs, lead1, lead2, sem):
    rows, cols, lanes = own.shape
    copies = []
    for number, out in ((1, lead2), (0, lead1)):
        start = jnp.where(info[1] == number, rows - 1, 0)
        copies.append(pltpu.make_async_copy(own.at[start], out.at[pl.ds(0, cols), :], sem.at[number, 0]))
        for n in range(cols // lanes):
            place = pl.ds(cols + n * costs.shape[0], costs.shape[0])
            copies.append(
                pltpu.make_async_copy(costs.at[:, pl.ds(n * lanes, lanes)], out.at[place, :], sem.at[number, n + 1])
            )
    for copy in copies:
        copy.start()
    for copy in copies:
        copy.wait()


def spread_kernel(picks, table, out_ref, sem):
    rest = jnp.zeros((128 - table.shape[0], CH), F32)

    def body(c0):
        block = jnp.concatenate([table[:, pl.ds(c0, CH)], rest]).T
        for n, lane in enumerate(picks):
            out_ref[n, pl.ds(c0, CH), :] = jnp.broadcast_to(block[:, lane : lane + 1], (CH, 128))

    chunks(table.shape[1], body)


def first_kernel(info, own, lead1, lead2, more1, more2, anchors, demand, cost, g_out, d_out, lab_out, sums, labels, buf, sem):
    cols = own.shape[1]
    rows = 8 + 2 * FIRST
    odd = info[1]
    north_of = (odd, 1 - odd)
    loads = []
    for i in range(8):
        loads.append((own, i, FIRST + i))
    for lead, more, north in ((lead1, more1, north_of[0]), (lead2, more2, north_of[1])):
        loads.append((lead, None, FIRST + 8 - north * 9))
        for i in range(FIRST - 1):
            loads.append((more, i, (FIRST + 9) * (1 - north) + i))
    loads = [
        pltpu.make_async_copy(
            ref.at[pl.ds(0, cols), half_lanes(h)] if i is None else ref.at[i, :, half_lanes(h)],
            buf.at[at, h, pl.ds(PAD, cols), :],
            sem.at[n, h],
        )
        for n, (ref, i, at) in enumerate(loads)
        for h in range(2)
    ]
    for copy in loads:
        copy.start()
    sums[...] = jnp.zeros(sums.shape, F32)
    clear_pads(buf, rows, cols)
    for copy in loads:
        copy.wait()

    def mark(i, carry):
        node0 = (info[0] + i - FIRST) * cols

        def body(c0):
            here = pl.ds(c0 + PAD, CH)
            for h in range(2):
                buf[i, h, here, :] = anchored(buf[i, h, here, :], anchors[:, half_lanes(h)], node0 + c0)

        chunks(cols, body)
        return carry

    lax.fori_loop(0, rows, mark, 0)
    for t in range(1, STEPS + 1):
        have = rows - 2 * (t - 1)
        for side in range(2):
            at, inner = (0, 1) if side == 0 else (have - 1, have - 2)
            j = 4 * (row_of(side, t - FIRST - 1) + EDGE)

            def edge(c0, side=side, at=at, inner=inner, j=j, t=t):
                here, mid = pl.ds(c0, CH), pl.ds(c0 + PAD, CH)
                west, east, within = (cost[j + k, here, :] for k in (WEST, EAST, INNER_SIDE[side]))
                for h in range(2):
                    centre = buf[at, h, mid, :]
                    g_out[side * STEPS + t - 1, h, here, :] = jnp.minimum(
                        jnp.minimum(centre, buf[at, h, pl.ds(c0 + PAD - 1, CH), :] + west),
                        jnp.minimum(buf[at, h, pl.ds(c0 + PAD + 1, CH), :] + east, buf[inner, h, mid, :] + within),
                    )
                    d_out[side * STEPS + t - 1, h, here, :] = centre

            chunks(cols, edge)

        def row(i, carry, t=t):
            j = 4 * (i + t - FIRST + EDGE)

            def body(c0):
                here, mid = pl.ds(c0, CH), pl.ds(c0 + PAD, CH)
                west, east, up, down = (cost[j + k, here, :] for k in (WEST, EAST, NORTH, SOUTH))
                for h in range(2):
                    buf[i, h, mid, :] = jnp.minimum(
                        jnp.minimum(
                            jnp.minimum(buf[i + 1, h, mid, :], buf[i + 1, h, pl.ds(c0 + PAD - 1, CH), :] + west),
                            jnp.minimum(buf[i + 1, h, pl.ds(c0 + PAD + 1, CH), :] + east, buf[i, h, mid, :] + up),
                        ),
                        buf[i + 2, h, mid, :] + down,
                    )

            chunks(cols, body)
            return carry

        lax.fori_loop(0, have - 2, row, 0)

    done = 2 * FIRST - 4
    first_done = STEPS - FIRST
    stores = [
        pltpu.make_async_copy(
            buf.at[r, h, pl.ds(PAD, cols), :], labels.at[r + first_done, :, half_lanes(h)], sem.at[r, h]
        )
        for r in range(done)
        for h in range(2)
    ]
    for copy in stores:
        copy.start()

    def final(c0):
        for r in range(done):
            for h in range(2):
                value = buf[r, h, pl.ds(c0 + PAD, CH), :]
                for n, kept in enumerate((0, done - 1)):
                    if r == kept:
                        lab_out[n, pl.ds(c0, CH), half_lanes(h)] = value
                buf[r + done, h, pl.ds(c0 + PAD, CH), :] = jnp.exp(-temper * value)

    chunks(cols, final)

    def link(c0):
        piece = c0 // CH
        mid = pl.ds(c0 + PAD, CH)
        for r in range(done):
            inv = [demand[:, half_lanes(h)] * jnp.exp(temper * buf[r, h, mid, :]) for h in range(2)]

            def add(side, shift, other, inv=inv, r=r):
                terms = [inv[h] * buf[other + done, h, pl.ds(c0 + PAD + shift, CH), :] for h in range(2)]
                add_lane_sum(sums, side, r + first_done, piece, terms[0] + terms[1])

            add(WEST, -1, r)
            add(EAST, 1, r)
            if r > 0:
                add(NORTH, 0, r - 1)
            if r < done - 1:
                add(SOUTH, 0, r + 1)

    chunks(cols, link)
    for copy in stores:
        copy.wait()


def pick(got1, got2, odd, side, place, here, lanes):
    at = got1.shape[0] - 1 - place if side == 0 else place
    one, two = got1[at, here, lanes], got2[at, here, lanes]
    return jnp.where(odd, one, two) if side == 0 else jnp.where(odd, two, one)


def next_kernel(depth, place, last, *refs):
    info, got1, got2, anchors, demand, cost, g_in, d_in, in_lab, sums_in, _ = refs[:11]
    if last:
        far_out, lab_out, sums, labels, dbuf, ebuf, sem = refs[11:]
    else:
        g_out, d_out, lab_out, sums, labels, dbuf, ebuf, sem = refs[11:]
    cols = got1.shape[1]
    odd = info[1] > 0
    at_rows = tuple(row_of(side, STEPS - depth) for side in range(2))
    sums[...] = sums_in[...]
    stores = [pltpu.make_async_copy(lab_out.at[n], labels.at[at_rows[n]], sem.at[n]) for n in range(2)]
    clear_pads(dbuf, STEPS, cols)
    clear_pads(ebuf, 1, cols)
    for side in range(2):
        within = 0 if side == 0 else in_lab.shape[0] - 1
        node0 = (info[0] + row_of(side, -depth)) * cols

        def chain(c0, side=side, node0=node0):
            here, mid = pl.ds(c0, CH), pl.ds(c0 + PAD, CH)
            values = []
            for h in range(2):
                values.append(anchored(pick(got1, got2, odd, side, place, here, half_lanes(h)), anchors[:, half_lanes(h)], node0 + c0))
                dbuf[0, h, mid, :] = values[h]
            for t in range(1, STEPS + 1):
                outer = cost[4 * cost_row(side, t - depth) + OUTER[side], here, :]
                for h in range(2):
                    values[h] = jnp.minimum(g_in[side * STEPS + t - 1, h, here, :], values[h] + outer)
                    if t < STEPS:
                        dbuf[t, h, mid, :] = values[h]
            for h in range(2):
                lab_out[side, here, half_lanes(h)] = values[h]
                ebuf[0, h, mid, :] = jnp.exp(-temper * values[h])

        chunks(cols, chain)
        stores[side].start()

        def ahead(c0, side=side):
            here, mid = pl.ds(c0, CH), pl.ds(c0 + PAD, CH)
            best = [None, None]
            for t in range(1, STEPS + 1):
                j = 4 * cost_row(side, t - depth - 1)
                west, east, inner = (cost[j + k, here, :] for k in (WEST, EAST, INNER_SIDE[side]))
                outer = cost[j + OUTER[side], here, :] if last and t > 1 else None
                for h in range(2):
                    centre = dbuf[t - 1, h, mid, :]
                    found = jnp.minimum(
                        jnp.minimum(centre, dbuf[t - 1, h, pl.ds(c0 + PAD - 1, CH), :] + west),
                        jnp.minimum(
                            dbuf[t - 1, h, pl.ds(c0 + PAD + 1, CH), :] + east,
                            d_in[side * STEPS + t - 1, h, here, :] + inner,
                        ),
                    )
                    if not last:
                        g_out[side * STEPS + t - 1, h, here, :] = found
                        d_out[side * STEPS + t - 1, h, here, :] = centre
                    else:
                        best[h] = found if t == 1 else jnp.minimum(found, best[h] + outer)
            if last:
                for h in range(2):
                    far_out[side, h, here, :] = best[h]

        chunks(cols, ahead)

        def link(c0, side=side, within=within):
            here, mid = pl.ds(c0, CH), pl.ds(c0 + PAD, CH)
            piece = c0 // CH
            at = at_rows[side]
            inside = row_of(side, STEPS - depth + 1)
            terms = [0.0] * 4
            for h in range(2):
                dem = demand[:, half_lanes(h)]
                inv = dem * jnp.exp(temper * lab_out[side, here, half_lanes(h)])
                other = in_lab[within, here, half_lanes(h)]
                terms[0] += inv * ebuf[0, h, pl.ds(c0 + PAD - 1, CH), :]
                terms[1] += inv * ebuf[0, h, pl.ds(c0 + PAD + 1, CH), :]
                terms[2] += inv * jnp.exp(-temper * other)
                terms[3] += dem * jnp.exp(temper * other) * ebuf[0, h, mid, :]
            add_lane_sum(sums, WEST, at, piece, terms[0])
            add_lane_sum(sums, EAST, at, piece, terms[1])
            add_lane_sum(sums, INNER_SIDE[side], at, piece, terms[2])
            add_lane_sum(sums, OUTER[side], inside, piece, terms[3])

        chunks(cols, link)

    for copy in stores:
        copy.wait()


def cross_kernel(depth, info, got1, got2, anchors, demand, cost, far_in, lab, sums_in, sums, sem):
    cols = got1.shape[1]
    odd = info[1] > 0
    sums[...] = sums_in[...]

    def body(c0):
        here = pl.ds(c0, CH)
        for side in range(2):
            node0 = (info[0] + row_of(side, -depth)) * cols
            terms = 0.0
            for h in range(2):
                lanes = half_lanes(h)
                value = pick(got1, got2, odd, side, 0, here, lanes)
                value = anchored(value, anchors[:, lanes], node0 + c0) + cost[4 * cost_row(side, -EDGE) + OUTER[side], here, :]
                value = jnp.minimum(value, far_in[side, h, here, :])
                terms += demand[:, lanes] * jnp.exp(temper * (lab[side, here, lanes] - value))
            add_lane_sum(sums, OUTER[side], row_of(side, 0), c0 // CH, terms)

    chunks(cols, body)


VM = pl.BlockSpec(memory_space=pltpu.VMEM)
SM = pl.BlockSpec(memory_space=pltpu.SMEM)
HB = pl.BlockSpec(memory_space=pltpu.HBM)


def kernel_call(body, outs, scratch, limit, specs, args, aliases=None, sems=(4,)):
    return pl.pallas_call(
        body,
        out_shape=[
            jax.ShapeDtypeStruct(shape, F32) if spec is HB else pltpu.VMEM(shape, F32) for shape, spec in outs
        ],
        in_specs=specs,
        out_specs=[spec for _, spec in outs],
        scratch_shapes=[pltpu.VMEM(s, F32) for s in scratch] + [pltpu.SemaphoreType.DMA(sems)],
        compiler_params=pltpu.CompilerParams(vmem_limit_bytes=limit),
        cost_estimate=pl.CostEstimate(flops=1 << 20, bytes_accessed=32 << 20, transcendentals=0),
        input_output_aliases=aliases or {},
    )(*(pltpu.with_memory_space_constraint(v, pltpu.HBM) if spec is HB else v for v, spec in zip(args, specs)))


def local(warm, link_costs, anchor_nodes, demand):
    rows, cols, lanes = warm.shape
    count = lax.axis_size("blk")
    me = lax.axis_index("blk")
    swaps = [[(i + a, i + 1 - a) for i in range(first, count - 1, 2) for a in (0, 1)] for first in (0, 1)]
    odd = me % 2
    own = warm

    def swap(number, message):
        return lax.ppermute(message, "blk", swaps[number])

    def cut(array, number, first, size, axis):
        low, high = first - 1, rows - first - size + 1
        start = jnp.where(odd == number, high, low)
        return lax.dynamic_slice_in_dim(array, start, size, axis)

    info = jnp.stack([me * rows, odd]).astype(jnp.int32)
    flat_costs = link_costs.reshape(4 * rows, cols)
    message = ((cols + 4 * rows * cols // lanes, lanes), VM)
    lead = kernel_call(
        lead_kernel, [message] * 2, [], 1 << 20, [SM, HB, HB], (info, warm, flat_costs), sems=(2, 1 + cols // lanes)
    )
    got_lead = [swap(number, lead[number]) for number in range(2)]
    warm, lead = lax.optimization_barrier((warm, lead))

    def exchange(first, size):
        return [swap(number, cut(warm, number, first, size, 0)) for number in range(2)]

    near = [*got_lead, *exchange(2, FIRST - 1)]
    later = {k: exchange(k, SECOND if k == FIRST + 1 else 1) for k in (FIRST + 1, STEPS, STEPS + 1)}
    got_costs = [
        jnp.concatenate([m[n : n + 4 * rows] for n in range(cols, m.shape[0], 4 * rows)], axis=1) for m in got_lead
    ]
    cost_n = jnp.where(odd == 1, got_costs[0], got_costs[1]).reshape(4, rows, cols)
    cost_s = jnp.where(odd == 1, got_costs[1], got_costs[0]).reshape(4, rows, cols)

    row = (me * rows + jnp.arange(rows))[:, None]
    col = jnp.arange(cols)[None, :]
    wide = (rows, cols)
    wall = jnp.stack(
        [
            jnp.broadcast_to(col == 0, wide),
            jnp.broadcast_to(col == cols - 1, wide),
            jnp.broadcast_to(row == 0, wide),
            jnp.broadcast_to(row == rows * count - 1, wide),
        ]
    )
    own_costs = jnp.where(wall, far_value, link_costs)
    sides = ((col == 0)[None], (col == cols - 1)[None])
    cost_n, cost_s = (
        jnp.concatenate([*(jnp.where(w, far_value, c[k : k + 1]) for k, w in enumerate(sides)), c[2:]]) for c in (cost_n, cost_s)
    )
    cost_n = cost_n.at[NORTH, rows - EDGE].set(cost_n[NORTH, rows - EDGE :].sum(axis=0))
    cost_s = cost_s.at[SOUTH, EDGE - 1].set(cost_s[SOUTH, :EDGE].sum(axis=0))
    table = jnp.concatenate([cost_n, own_costs, cost_s], axis=1).reshape(-1, cols)
    total = 3 * rows
    used = [k * total + r for r in range(rows - EDGE, 2 * rows + EDGE) for k in range(4)]
    anc = anchor_nodes.reshape(1, lanes)
    dem = demand.reshape(1, lanes)
    owners = lax.axis_size("org")
    width = cols // owners
    mine = lax.dynamic_slice_in_dim(own_costs, lax.axis_index("org") * width, width, axis=2)
    scale = jnp.exp(-temper * mine) / ANCHORS
    table, info, anc, dem, scale = lax.optimization_barrier((table, info, anc, dem, scale))
    (cost,) = kernel_call(
        functools.partial(spread_kernel, used), [((len(used), cols, 128), VM)], [], 1 << 20, [VM], (table,)
    )
    diag = ((2 * STEPS, 2, cols, 128), VM)
    padded = cols + 2 * PAD
    pieces = ((cols // CH, 4 * rows, CH), VM)
    whole = (warm.shape, HB)
    g, d, lab, sums, labels = kernel_call(
        first_kernel,
        [diag, diag, ((2, cols, lanes), VM), pieces, whole],
        [(rows + 2 * FIRST, 2, padded, 128)],
        7680 << 10, [SM] + [HB] * 5 + [VM] * 3, (info, own, *near, anc, dem, cost),
        sems=(rows + 2 * FIRST, 2),
    )
    for place in range(SECOND):
        depth = FIRST + 1 + place
        g, d, lab, sums, labels = kernel_call(
            functools.partial(next_kernel, depth, place, False),
            [diag, diag, ((2, cols, lanes), VM), pieces, whole],
            [(STEPS, 2, padded, 128), (1, 2, padded, 128)],
            5 << 20, [SM] + [VM] * 9 + [HB],
            (info, *later[FIRST + 1], anc, dem, cost, g, d, lab, sums, labels),
            {6: 0, 7: 1, 10: 4},
        )
    far, lab, sums, labels = kernel_call(
        functools.partial(next_kernel, STEPS, 0, True),
        [((2, 2, cols, 128), VM), ((2, cols, lanes), VM), pieces, whole],
        [(STEPS, 2, padded, 128), (1, 2, padded, 128)],
        5 << 20, [SM] + [VM] * 9 + [HB], (info, *later[STEPS], anc, dem, cost, g, d, lab, sums, labels), {10: 3},
    )
    (sums,) = kernel_call(
        functools.partial(cross_kernel, STEPS + 1), [pieces], [],
        2 << 20, [SM] + [VM] * 8, (info, *later[STEPS + 1], anc, dem, cost, far, lab, sums),
    )
    total, bit, at = sums, 1, lax.axis_index("org")
    while bit < owners:
        pairs = total.reshape(-1, 2, 4 * rows, CH)
        mine = at // bit % 2
        keep, send = (lax.dynamic_index_in_dim(pairs, n, 1, False) for n in (mine, 1 - mine))
        total = keep + lax.ppermute(send, "org", [(i, i ^ bit) for i in range(owners)])
        bit *= 2
    return labels, total.reshape(4, rows, width) * scale


def solution(mesh):
    placed = (P("blk", None, "org"), P(None, "blk", None), P("org"), P("org"))
    return jax.shard_map(
        local,
        mesh=mesh,
        in_specs=placed,
        out_specs=(P("blk", None, "org"), P(None, "blk", "org")),
        check_vma=False,
    )
```

profile of v0, /device:TPU:6, one launch (start us, length us, event | category | flops | bytes accessed | tf_op | source)
XLA Modules:
  0.0 121.3 jit_solution(12553499000837341459)
XLA Ops:
  0.6 0.1 pad_add_fusion.info.refs_0_
  0.7 1.8 %shard_map.59 = (f32[576,256]{1,0:T(8,128)S(1)}, f32[576,256]{1,0:T(8,128)S(1)}) custom-call(s32[2]{0:T(128)S(1)} %pad_add_fusion.info.refs_0_, f32[8,512,256]{2,1,0:T(8,128)} %own.3, f32[32,512]{1,0:T(8,128)} %bitcast.40), custom_call_target="tpu_custom_call" | custom-call | flops 1048576 | bytes 33554432 | tf_op jit(solution)/shard_map/pallas_call | solution.py:336
  2.6 1.7 %collective-permute-start = (f32[576,256]{1,0:T(8,128)S(1)}, f32[576,256]{1,0:T(8,128)S(1)}, u32[]{:S(2)}, u32[]{:S(2)}) collective-permute-start(f32[576,256]{1,0:T(8,128)S(1)} %get-tuple-element.53), channel_id=1, source_target_pairs={{0,4},{4,0},{8,12},{12,8},{16,20},{20,16},{24,28},{28,24},{32,36},... | collective-permute-start | bytes 1769480 | tf_op jit(solution)/shard_map/ppermute | solution.py:359
  4.2 7.7 %collective-permute-start.1 = (f32[576,256]{1,0:T(8,128)S(1)}, f32[576,256]{1,0:T(8,128)}, u32[]{:S(2)}, u32[]{:S(2)}) collective-permute-start(f32[576,256]{1,0:T(8,128)S(1)} %get-tuple-element.54), channel_id=1, source_target_pairs={{4,8},{8,4},{12,16},{16,12},{20,24},{24,20},{28,32},{32,28},{36,40... | collective-permute-start | bytes 1769480 | tf_op jit(solution)/shard_map/ppermute | solution.py:359
  11.9 3.6 %constant_dynamic-slice_fusion.3 = (f32[2,512,256]{2,1,0:T(8,128)}, f32[2,512,256]{2,1,0:T(8,128)}, f32[2,512,256]{2,1,0:T(8,128)}) fusion(f32[8,512,256]{2,1,0:T(8,128)} %own.3, s32[]{:T(128)S(6)} %select_n.124, s32[]{:T(128)S(6)} %select_n.123), kind=kLoop, calls=%fused_computation.27 | loop fusion | bytes 6291464 | tf_op jit(solution)/shard_map/dynamic_slice | solution.py:364
  15.5 3.2 %collective-permute-start.7 = (f32[2,512,256]{2,1,0:T(8,128)}, f32[2,512,256]{2,1,0:T(8,128)}, u32[]{:S(2)}, u32[]{:S(2)}) collective-permute-start(f32[2,512,256]{2,1,0:T(8,128)} %get-tuple-element.84), channel_id=1, source_target_pairs={{4,8},{8,4},{12,16},{16,12},{20,24},{24,20},{28,32},{32,28},{36,40... | collective-permute-start | bytes 3145736 | tf_op jit(solution)/shard_map/ppermute | solution.py:359
  18.7 1.0 collective-permute-start.4
  19.7 2.9 %constant_dynamic-slice_fusion.1 = (f32[1,512,256]{2,1,0:T(8,128)}, f32[1,512,256]{2,1,0:T(8,128)}, f32[1,512,256]{2,1,0:T(8,128)}, f32[1,512,256]{2,1,0:T(8,128)}) fusion(f32[8,512,256]{2,1,0:T(8,128)} %own.3, s32[]{:T(128)S(6)} %select_n.126, s32[]{:T(128)S(6)} %select_n.125, s32[]{:T(128)S(6)} %select_n.122, s32[]{:T(128)S(6)} %select_n.121), kind=kLoop, calls=%fused_computation.25 | loop fusion | bytes 4194320 | tf_op jit(solution)/shard_map/dynamic_slice | solution.py:364
  22.6 0.1 stack_broadcast_in_dim.10
  22.7 0.1 stack_broadcast_in_dim.11
  22.8 6.3 %collective-permute-start.5 = (f32[2,512,256]{2,1,0:T(8,128)}, f32[2,512,256]{2,1,0:T(8,128)S(1)}, u32[]{:S(2)}, u32[]{:S(2)}) collective-permute-start(f32[2,512,256]{2,1,0:T(8,128)} %get-tuple-element.86), channel_id=1, source_target_pairs={{4,8},{8,4},{12,16},{16,12},{20,24},{24,20},{28,32},{32,28},{36,40... | collective-permute-start | bytes 3145736 | tf_op jit(solution)/shard_map/ppermute | solution.py:359
  29.2 0.1 collective-permute-start.2
  29.2 0.8 fusion.9
  30.1 11.8 %collective-permute-done.6.more1 = f32[2,512,256]{2,1,0:T(8,128)} collective-permute-done((f32[2,512,256]{2,1,0:T(8,128)}, f32[2,512,256]{2,1,0:T(8,128)}, u32[]{:S(2)}, u32[]{:S(2)}) %collective-permute-start.6) | collective-permute-done | bytes 1048608 | tf_op jit(solution)/shard_map/ppermute | solution.py:359
  41.9 8.1 %collective-permute-start.3 = (f32[1,512,256]{2,1,0:T(8,128)}, f32[1,512,256]{2,1,0:T(8,128)}, u32[]{:S(2)}, u32[]{:S(2)}) collective-permute-start(f32[1,512,256]{2,1,0:T(8,128)} %get-tuple-element.82), channel_id=1, source_target_pairs={{4,8},{8,4},{12,16},{16,12},{20,24},{24,20},{28,32},{32,28},{36,40... | collective-permute-start | bytes 1572872 | tf_op jit(solution)/shard_map/ppermute | solution.py:359
  49.9 0.1 collective-permute-start.8
  50.0 14.2 %collective-permute-done.4.refs_1_ = f32[2,512,256]{2,1,0:T(8,128)S(1)} collective-permute-done((f32[2,512,256]{2,1,0:T(8,128)}, f32[2,512,256]{2,1,0:T(8,128)S(1)}, u32[]{:S(2)}, u32[]{:S(2)}) %collective-permute-start.4) | collective-permute-done | bytes 1048608 | tf_op jit(solution)/shard_map/ppermute | solution.py:359
  64.2 8.1 %collective-permute-start.9 = (f32[1,512,256]{2,1,0:T(8,128)}, f32[1,512,256]{2,1,0:T(8,128)}, u32[]{:S(2)}, u32[]{:S(2)}) collective-permute-start(f32[1,512,256]{2,1,0:T(8,128)} %get-tuple-element.80), channel_id=1, source_target_pairs={{4,8},{8,4},{12,16},{16,12},{20,24},{24,20},{28,32},{32,28},{36,40... | collective-permute-start | bytes 1572872 | tf_op jit(solution)/shard_map/ppermute | solution.py:359
  72.3 0.1 scatter.6
  72.4 0.1 scatter.9
  72.5 0.0 copy-start.1
  72.5 6.7 %shard_map.60.cost.refs_5_ = f32[80,512,128]{2,1,0:T(8,128)S(1)} custom-call(f32[96,512]{1,0:T(8,128)S(1)} %bitcast.27), custom_call_target="tpu_custom_call" | custom-call | flops 1048576 | bytes 33554432 | tf_op jit(solution)/shard_map/pallas_call | solution.py:336
  79.2 17.2 %shard_map.61 = (f32[12,2,512,128]{3,2,1,0:T(8,128)S(1)}, f32[12,2,512,128]{3,2,1,0:T(8,128)S(1)}, f32[2,512,256]{2,1,0:T(8,128)S(1)}, f32[4,32,128]{2,1,0:T(8,128)S(1)}, f32[8,512,256]{2,1,0:T(8,128)}) custom-call(s32[2]{0:T(128)S(1)} %pad_add_fusion.info.refs_0_, f32[8,512,256]{2,1,0:T(8,128)} %own.3, f32[576,256]{1,0:T(8,128)} %copy-done.2, ...), custom_call_target="tpu_custom_call" | custom-call | flops 1048576 | bytes 33554432 | tf_op jit(solution)/shard_map/pallas_call | solution.py:336
  96.5 5.6 %shard_map.62 = (f32[12,2,512,128]{3,2,1,0:T(8,128)S(1)}, f32[12,2,512,128]{3,2,1,0:T(8,128)S(1)}, f32[2,512,256]{2,1,0:T(8,128)S(1)}, f32[4,32,128]{2,1,0:T(8,128)S(1)}, f32[8,512,256]{2,1,0:T(8,128)}) custom-call(s32[2]{0:T(128)S(1)} %pad_add_fusion.info.refs_0_, ...), custom_call_target="tpu_custom_call", output_to_operand_aliasing={{0}: (6, {}), {1}: (7, {}), {4}: (10, {})} | custom-call | flops 1048576 | bytes 33554432 | tf_op jit(solution)/shard_map/pallas_call | solution.py:336
  102.1 5.6 %shard_map.63 = (f32[12,2,512,128]{3,2,1,0:T(8,128)S(1)}, f32[12,2,512,128]{3,2,1,0:T(8,128)S(1)}, f32[2,512,256]{2,1,0:T(8,128)S(1)}, f32[4,32,128]{2,1,0:T(8,128)S(1)}, f32[8,512,256]{2,1,0:T(8,128)}) custom-call(s32[2]{0:T(128)S(1)} %pad_add_fusion.info.refs_0_, ...), custom_call_target="tpu_custom_call", output_to_operand_aliasing={{0}: (6, {}), {1}: (7, {}), {4}: (10, {})} | custom-call | flops 1048576 | bytes 33554432 | tf_op jit(solution)/shard_map/pallas_call | solution.py:336
  107.8 5.8 %shard_map.64 = (f32[2,2,512,128]{3,2,1,0:T(8,128)S(1)}, f32[2,512,256]{2,1,0:T(8,128)S(1)}, f32[4,32,128]{2,1,0:T(8,128)S(1)}, f32[8,512,256]{2,1,0:T(8,128)}) custom-call(s32[2]{0:T(128)S(1)} %pad_add_fusion.info.refs_0_, f32[1,512,256]{2,1,0:T(8,128)S(1)} %collective-permute-done.2.refs_1_, ...), custom_call_target="tpu_custom_call", output_to_operand_aliasing={{3}: (10, {})} | custom-call | flops 1048576 | bytes 33554432 | tf_op jit(solution)/shard_map/pallas_call | solution.py:336
  113.6 2.0 %shard_map.65 = f32[4,32,128]{2,1,0:T(8,128)S(1)} custom-call(s32[2]{0:T(128)S(1)} %pad_add_fusion.info.refs_0_, f32[1,512,256]{2,1,0:T(8,128)} %collective-permute-done.8.got1, f32[1,512,256]{2,1,0:T(8,128)} %collective-permute-done.9.got2, s32[1,256]{1,0:T(1,128)S(1)} %bitcast.34, f32[1,256]{1,0:T(1,128)S(1)} %bitcast.39, ...), custom_call_target="tpu_custom_call" | custom-call | flops 1048576 | bytes 33554432 | tf_op jit(solution)/shard_map/pallas_call | solution.py:336
  115.6 0.1 collective-permute-start.10
  115.7 1.2 collective-permute-done.10
  116.9 1.1 collective-permute-start.11
  118.0 2.7 %collective-permute-done.11 = f32[1,32,128]{2,1,0:T(8,128)S(1)} collective-permute-done((f32[1,32,128]{2,1,0:T(8,128)S(1)}, f32[1,32,128]{2,1,0:T(8,128)S(1)}, u32[]{:S(2)}, u32[]{:S(2)}) %collective-permute-start.11) | collective-permute-done | bytes 16416 | tf_op jit(solution)/shard_map/ppermute | solution.py:453
  120.7 0.6 bitcast_multiply_fusion
  (34 shorter events, 0.2 us)
Async XLA Ops:
  2.6 20.2 %copy-start.3 = (f32[4,8,512]{2,1,0:T(8,128)S(1)}, f32[4,8,512]{2,1,0:T(8,128)}, u32[]{:S(2)}) copy-start(f32[4,8,512]{2,1,0:T(8,128)} %param.9) | copy-start | bytes 196612
  2.6 20.3 %collective-permute-start = (f32[576,256]{1,0:T(8,128)S(1)}, f32[576,256]{1,0:T(8,128)S(1)}, u32[]{:S(2)}, u32[]{:S(2)}) collective-permute-start(f32[576,256]{1,0:T(8,128)S(1)} %get-tuple-element.53), channel_id=1, source_target_pairs={{0,4},{4,0},{8,12},{12,8},{16,20},{20,16},{24,28},{28,24},{32,36},... | collective-permute-start | bytes 1769480 | tf_op jit(solution)/shard_map/ppermute | solution.py:359
  4.2 24.9 %collective-permute-start.1 = (f32[576,256]{1,0:T(8,128)S(1)}, f32[576,256]{1,0:T(8,128)}, u32[]{:S(2)}, u32[]{:S(2)}) collective-permute-start(f32[576,256]{1,0:T(8,128)S(1)} %get-tuple-element.54), channel_id=1, source_target_pairs={{4,8},{8,4},{12,16},{16,12},{20,24},{24,20},{28,32},{32,28},{36,40... | collective-permute-start | bytes 1769480 | tf_op jit(solution)/shard_map/ppermute | solution.py:359
  15.5 26.3 %collective-permute-start.6 = (f32[2,512,256]{2,1,0:T(8,128)}, f32[2,512,256]{2,1,0:T(8,128)}, u32[]{:S(2)}, u32[]{:S(2)}) collective-permute-start(f32[2,512,256]{2,1,0:T(8,128)} %get-tuple-element.85), channel_id=1, source_target_pairs={{0,4},{4,0},{8,12},{12,8},{16,20},{20,16},{24,28},{28,24},{32,36},... | collective-permute-start | bytes 3145736 | tf_op jit(solution)/shard_map/ppermute | solution.py:359
  15.5 34.4 %collective-permute-start.7 = (f32[2,512,256]{2,1,0:T(8,128)}, f32[2,512,256]{2,1,0:T(8,128)}, u32[]{:S(2)}, u32[]{:S(2)}) collective-permute-start(f32[2,512,256]{2,1,0:T(8,128)} %get-tuple-element.84), channel_id=1, source_target_pairs={{4,8},{8,4},{12,16},{16,12},{20,24},{24,20},{28,32},{32,28},{36,40... | collective-permute-start | bytes 3145736 | tf_op jit(solution)/shard_map/ppermute | solution.py:359
  18.7 45.5 %collective-permute-start.4 = (f32[2,512,256]{2,1,0:T(8,128)}, f32[2,512,256]{2,1,0:T(8,128)S(1)}, u32[]{:S(2)}, u32[]{:S(2)}) collective-permute-start(f32[2,512,256]{2,1,0:T(8,128)} %get-tuple-element.86), channel_id=1, source_target_pairs={{0,4},{4,0},{8,12},{12,8},{16,20},{20,16},{24,28},{28,24},{32,36},... | collective-permute-start | bytes 3145736 | tf_op jit(solution)/shard_map/ppermute | solution.py:359
  22.8 56.4 %copy-start.2 = (f32[576,256]{1,0:T(8,128)}, f32[576,256]{1,0:T(8,128)S(1)}, u32[]{:S(2)}) copy-start(f32[576,256]{1,0:T(8,128)S(1)} %collective-permute-done.lead1) | copy-start | bytes 1769476
  22.8 73.6 %collective-permute-start.5 = (f32[2,512,256]{2,1,0:T(8,128)}, f32[2,512,256]{2,1,0:T(8,128)S(1)}, u32[]{:S(2)}, u32[]{:S(2)}) collective-permute-start(f32[2,512,256]{2,1,0:T(8,128)} %get-tuple-element.86), channel_id=1, source_target_pairs={{4,8},{8,4},{12,16},{16,12},{20,24},{24,20},{28,32},{32,28},{36,40... | collective-permute-start | bytes 3145736 | tf_op jit(solution)/shard_map/ppermute | solution.py:359
  29.2 78.6 %collective-permute-start.2 = (f32[1,512,256]{2,1,0:T(8,128)}, f32[1,512,256]{2,1,0:T(8,128)S(1)}, u32[]{:S(2)}, u32[]{:S(2)}) collective-permute-start(f32[1,512,256]{2,1,0:T(8,128)} %get-tuple-element.83), channel_id=1, source_target_pairs={{0,4},{4,0},{8,12},{12,8},{16,20},{20,16},{24,28},{28,24},{32,36},... | collective-permute-start | bytes 1572872 | tf_op jit(solution)/shard_map/ppermute | solution.py:359
  41.9 65.9 %collective-permute-start.3 = (f32[1,512,256]{2,1,0:T(8,128)}, f32[1,512,256]{2,1,0:T(8,128)}, u32[]{:S(2)}, u32[]{:S(2)}) collective-permute-start(f32[1,512,256]{2,1,0:T(8,128)} %get-tuple-element.82), channel_id=1, source_target_pairs={{4,8},{8,4},{12,16},{16,12},{20,24},{24,20},{28,32},{32,28},{36,40... | collective-permute-start | bytes 1572872 | tf_op jit(solution)/shard_map/ppermute | solution.py:359
  49.9 63.6 %collective-permute-start.8 = (f32[1,512,256]{2,1,0:T(8,128)}, f32[1,512,256]{2,1,0:T(8,128)}, u32[]{:S(2)}, u32[]{:S(2)}) collective-permute-start(f32[1,512,256]{2,1,0:T(8,128)} %get-tuple-element.81), channel_id=1, source_target_pairs={{0,4},{4,0},{8,12},{12,8},{16,20},{20,16},{24,28},{28,24},{32,36},... | collective-permute-start | bytes 1572872 | tf_op jit(solution)/shard_map/ppermute | solution.py:359
  64.2 49.3 %collective-permute-start.9 = (f32[1,512,256]{2,1,0:T(8,128)}, f32[1,512,256]{2,1,0:T(8,128)}, u32[]{:S(2)}, u32[]{:S(2)}) collective-permute-start(f32[1,512,256]{2,1,0:T(8,128)} %get-tuple-element.80), channel_id=1, source_target_pairs={{4,8},{8,4},{12,16},{16,12},{20,24},{24,20},{28,32},{32,28},{36,40... | collective-permute-start | bytes 1572872 | tf_op jit(solution)/shard_map/ppermute | solution.py:359
  72.5 6.7 %copy-start = (s32[256]{0:T(256)S(1)}, s32[256]{0:T(256)}, u32[]{:S(2)}) copy-start(s32[256]{0:T(256)} %param.10) | copy-start | bytes 3076
  72.5 6.7 %copy-start.1 = (f32[256]{0:T(256)S(1)}, f32[256]{0:T(256)}, u32[]{:S(2)}) copy-start(f32[256]{0:T(256)} %param.11) | copy-start | bytes 3076
  115.6 1.3 %collective-permute-start.10 = (f32[2,32,128]{2,1,0:T(8,128)S(1)}, f32[2,32,128]{2,1,0:T(8,128)S(1)}, u32[]{:S(2)}, u32[]{:S(2)}) collective-permute-start(f32[2,32,128]{2,1,0:T(8,128)S(1)} %dynamic-slice_bitcast_fusion), channel_id=1, source_target_pairs={{0,1},{1,0},{2,3},{3,2},{4,5},{5,4},{6,7},{7,6},{8,9},{9,8},{10,11... | collective-permute-start | bytes 98312 | tf_op jit(solution)/shard_map/ppermute | solution.py:453
  116.9 3.8 %collective-permute-start.11 = (f32[1,32,128]{2,1,0:T(8,128)S(1)}, f32[1,32,128]{2,1,0:T(8,128)S(1)}, u32[]{:S(2)}, u32[]{:S(2)}) collective-permute-start(f32[1,32,128]{2,1,0:T(8,128)S(1)} %constant_dynamic-slice_fusion), channel_id=1, source_target_pairs={{0,2},{1,3},{2,0},{3,1},{4,6},{5,7},{6,4},{7,5},{8,10},{9,11},{10,... | collective-permute-start | bytes 49160 | tf_op jit(solution)/shard_map/ppermute | solution.py:453
where the time goes:
time: 122 us; the launch traced here: 121 us
  Pallas kernels  44.8 us (37%)
  starting transfers between devices  37.2 us (30%)
  waiting for transfers between devices  29.9 us (25%)
  local copies, waits for them, and re-layouts  7.59 us (6%)
    pallas_call x7, Pallas kernels, kernel_call(): pl.pallas_call(body, out_shape=[jax.ShapeDtypeStruct(shape, F32) if spec...  44.8 us
    ppermute x10, starting transfers between devices, swap(): return lax.ppermute(message, 'blk', swaps[number])  36.1 us
    ppermute x10, waiting for transfers between devices, swap(): return lax.ppermute(message, 'blk', swaps[number])  26 us
    dynamic_slice x2, local copies, waits for them, and re-layouts, cut(): return lax.dynamic_slice_in_dim(array, start, size, axis)  6.47 us
    ppermute x2, waiting for transfers between devices, local(): lax.ppermute(send, 'org', [(i, i ^ bit) for i in range(owners)])  3.87 us
  transfers between devices with their start and end apart: 12, of which 4 were waited for; matrix products, arithmetic and copies ran while one was open for 6% of the time, Pallas kernels for 34%

commit v1 on v0

--- a/solution.py
+++ b/solution.py
@@ -306,7 +306,7 @@
         copy.wait()
 
 
-def cross_kernel(depth, info, got1, got2, anchors, demand, cost, far_in, lab, sums_in, sums, sem):
+def cross_kernel(depth, info, got1, got2, anchors, demand, path, far_in, lab, sums_in, sums, sem):
     cols = got1.shape[1]
     odd = info[1] > 0
     sums[...] = sums_in[...]
@@ -319,7 +319,7 @@
             for h in range(2):
                 lanes = half_lanes(h)
                 value = pick(got1, got2, odd, side, 0, here, lanes)
-                value = anchored(value, anchors[:, lanes], node0 + c0) + cost[4 * cost_row(side, -EDGE) + OUTER[side], here, :]
+                value = anchored(value, anchors[:, lanes], node0 + c0) + path[side, here, :]
                 value = jnp.minimum(value, far_in[side, h, here, :])
                 terms += demand[:, lanes] * jnp.exp(temper * (lab[side, here, lanes] - value))
             add_lane_sum(sums, OUTER[side], row_of(side, 0), c0 // CH, terms)
@@ -399,18 +399,18 @@
     cost_n, cost_s = (
         jnp.concatenate([*(jnp.where(w, far_value, c[k : k + 1]) for k, w in enumerate(sides)), c[2:]]) for c in (cost_n, cost_s)
     )
-    cost_n = cost_n.at[NORTH, rows - EDGE].set(cost_n[NORTH, rows - EDGE :].sum(axis=0))
-    cost_s = cost_s.at[SOUTH, EDGE - 1].set(cost_s[SOUTH, :EDGE].sum(axis=0))
+    path = jnp.stack([cost_n[NORTH, rows - EDGE :].sum(axis=0), cost_s[SOUTH, :EDGE].sum(axis=0)])
     table = jnp.concatenate([cost_n, own_costs, cost_s], axis=1).reshape(-1, cols)
     total = 3 * rows
     used = [k * total + r for r in range(rows - EDGE, 2 * rows + EDGE) for k in range(4)]
+    path_wide = jnp.broadcast_to(path[:, :, None], (2, cols, 128))
     anc = anchor_nodes.reshape(1, lanes)
     dem = demand.reshape(1, lanes)
     owners = lax.axis_size("org")
     width = cols // owners
     mine = lax.dynamic_slice_in_dim(own_costs, lax.axis_index("org") * width, width, axis=2)
     scale = jnp.exp(-temper * mine) / ANCHORS
-    table, info, anc, dem, scale = lax.optimization_barrier((table, info, anc, dem, scale))
+    table, path_wide, info, anc, dem, scale = lax.optimization_barrier((table, path_wide, info, anc, dem, scale))
     (cost,) = kernel_call(
         functools.partial(spread_kernel, used), [((len(used), cols, 128), VM)], [], 1 << 20, [VM], (table,)
     )
@@ -443,7 +443,7 @@
     )
     (sums,) = kernel_call(
         functools.partial(cross_kernel, STEPS + 1), [pieces], [],
-        2 << 20, [SM] + [VM] * 8, (info, *later[STEPS + 1], anc, dem, cost, far, lab, sums),
+        2 << 20, [SM] + [VM] * 8, (info, *later[STEPS + 1], anc, dem, path_wide, far, lab, sums),
     )
     total, bit, at = sums, 1, lax.axis_index("org")
     while bit < owners:

time: 122 us -> 125 us (1.025)
  Pallas kernels: 44.8 us -> 48.5 us
    pallas_call x7, Pallas kernels: 44.8 us -> 48.5 us  [kernel_call(): pl.pallas_call(body, out_shape=[jax.ShapeDtypeStruct(shape, F32) if spec...]
    dynamic_slice x2, local copies, waits for them, and re-layouts: 6.47 us -> 5.09 us  [cut(): return lax.dynamic_slice_in_dim(array, start, size, axis)]
  transfers between devices with their start and end apart: 12 -> 12, of which waited for: 4 -> 4; matrix products, arithmetic and copies ran while one was open for 6% -> 6% of each run, Pallas kernels for 34% -> 36%
where the time goes in v1:
time: 125 us
  Pallas kernels  48.5 us (39%)
  starting transfers between devices  37.6 us (30%)
  waiting for transfers between devices  30.1 us (24%)
  local copies, waits for them, and re-layouts  7.04 us (6%)
    pallas_call x7, Pallas kernels, kernel_call(): pl.pallas_call(body, out_shape=[jax.ShapeDtypeStruct(shape, F32) if spec...  48.5 us
    ppermute x10, starting transfers between devices, swap(): return lax.ppermute(message, 'blk', swaps[number])  36.4 us
    ppermute x10, waiting for transfers between devices, swap(): return lax.ppermute(message, 'blk', swaps[number])  26.2 us
    dynamic_slice x2, local copies, waits for them, and re-layouts, cut(): return lax.dynamic_slice_in_dim(array, start, size, axis)  5.09 us
    ppermute x2, waiting for transfers between devices, local(): lax.ppermute(send, 'org', [(i, i ^ bit) for i in range(owners)])  3.87 us
  transfers between devices with their start and end apart: 12, of which 4 were waited for; matrix products, arithmetic and copies ran while one was open for 6% of the time, Pallas kernels for 36%

profile of v1, /device:TPU:6, one launch (start us, length us, event | category | flops | bytes accessed | tf_op | source)
XLA Modules:
  0.0 125.1 jit_solution(11024525297281848441)
XLA Ops:
  0.7 0.1 pad_add_fusion.info.refs_0_
  0.7 1.8 %shard_map.59 = (f32[576,256]{1,0:T(8,128)S(1)}, f32[576,256]{1,0:T(8,128)S(1)}) custom-call(s32[2]{0:T(128)S(1)} %pad_add_fusion.info.refs_0_, f32[8,512,256]{2,1,0:T(8,128)} %own.3, f32[32,512]{1,0:T(8,128)} %bitcast.40), custom_call_target="tpu_custom_call" | custom-call | flops 1048576 | bytes 33554432 | tf_op jit(solution)/shard_map/pallas_call | solution.py:336
  2.6 1.7 %collective-permute-start = (f32[576,256]{1,0:T(8,128)S(1)}, f32[576,256]{1,0:T(8,128)}, u32[]{:S(2)}, u32[]{:S(2)}) collective-permute-start(f32[576,256]{1,0:T(8,128)S(1)} %get-tuple-element.30), channel_id=1, source_target_pairs={{0,4},{4,0},{8,12},{12,8},{16,20},{20,16},{24,28},{28,24},{32,36},... | collective-permute-start | bytes 1769480 | tf_op jit(solution)/shard_map/ppermute | solution.py:359
  4.2 7.7 %collective-permute-start.1 = (f32[576,256]{1,0:T(8,128)S(1)}, f32[576,256]{1,0:T(8,128)}, u32[]{:S(2)}, u32[]{:S(2)}) collective-permute-start(f32[576,256]{1,0:T(8,128)S(1)} %get-tuple-element.31), channel_id=1, source_target_pairs={{4,8},{8,4},{12,16},{16,12},{20,24},{24,20},{28,32},{32,28},{36,40... | collective-permute-start | bytes 1769480 | tf_op jit(solution)/shard_map/ppermute | solution.py:359
  11.9 3.4 %constant_dynamic-slice_fusion.3 = (f32[2,512,256]{2,1,0:T(8,128)}, f32[2,512,256]{2,1,0:T(8,128)}, f32[2,512,256]{2,1,0:T(8,128)S(1)}) fusion(f32[8,512,256]{2,1,0:T(8,128)} %own.3, s32[]{:T(128)S(6)} %select_n.124, s32[]{:T(128)S(6)} %select_n.123), kind=kLoop, calls=%fused_computation.26 | loop fusion | bytes 6291464 | tf_op jit(solution)/shard_map/dynamic_slice | solution.py:364
  15.3 3.2 %collective-permute-start.7 = (f32[2,512,256]{2,1,0:T(8,128)}, f32[2,512,256]{2,1,0:T(8,128)}, u32[]{:S(2)}, u32[]{:S(2)}) collective-permute-start(f32[2,512,256]{2,1,0:T(8,128)} %get-tuple-element.62), channel_id=1, source_target_pairs={{4,8},{8,4},{12,16},{16,12},{20,24},{24,20},{28,32},{32,28},{36,40... | collective-permute-start | bytes 3145736 | tf_op jit(solution)/shard_map/ppermute | solution.py:359
  18.5 1.0 collective-permute-start.4
  19.5 0.1 stack_broadcast_in_dim.10
  19.6 0.1 stack_broadcast_in_dim.11
  19.8 1.7 %constant_dynamic-slice_fusion.1 = (f32[1,512,256]{2,1,0:T(8,128)S(1)}, f32[1,512,256]{2,1,0:T(8,128)S(1)}, f32[1,512,256]{2,1,0:T(8,128)S(1)}, f32[1,512,256]{2,1,0:T(8,128)S(1)}) fusion(f32[8,512,256]{2,1,0:T(8,128)} %own.3, s32[]{:T(128)S(6)} %select_n.126, s32[]{:T(128)S(6)} %select_n.125, s32[]{:T(128)S(6)} %select_n.122, s32[]{:T(128)S(6)} %select_n.121), kind=kLoop, calls=%fused_computation.24 | loop fusion | bytes 4194320 | tf_op jit(solution)/shard_map/dynamic_slice | solution.py:364
  21.5 6.3 %collective-permute-start.5 = (f32[2,512,256]{2,1,0:T(8,128)S(1)}, f32[2,512,256]{2,1,0:T(8,128)S(1)}, u32[]{:S(2)}, u32[]{:S(2)}) collective-permute-start(f32[2,512,256]{2,1,0:T(8,128)S(1)} %get-tuple-element.64), channel_id=1, source_target_pairs={{4,8},{8,4},{12,16},{16,12},{20,24},{24,20},{28,32},{32,28},{36,40... | collective-permute-start | bytes 3145736 | tf_op jit(solution)/shard_map/ppermute | solution.py:359
  27.7 0.8 fusion.8
  28.5 0.1 collective-permute-start.2
  28.6 0.8 fusion.9
  29.5 12.2 %collective-permute-done.6.more1 = f32[2,512,256]{2,1,0:T(8,128)} collective-permute-done((f32[2,512,256]{2,1,0:T(8,128)}, f32[2,512,256]{2,1,0:T(8,128)}, u32[]{:S(2)}, u32[]{:S(2)}) %collective-permute-start.6) | collective-permute-done | bytes 1048608 | tf_op jit(solution)/shard_map/ppermute | solution.py:359
  41.7 8.2 %collective-permute-start.3 = (f32[1,512,256]{2,1,0:T(8,128)S(1)}, f32[1,512,256]{2,1,0:T(8,128)S(1)}, u32[]{:S(2)}, u32[]{:S(2)}) collective-permute-start(f32[1,512,256]{2,1,0:T(8,128)S(1)} %get-tuple-element.60), channel_id=1, source_target_pairs={{4,8},{8,4},{12,16},{16,12},{20,24},{24,20},{28,32},{32,28},{36,40... | collective-permute-start | bytes 1572872 | tf_op jit(solution)/shard_map/ppermute | solution.py:359
  49.9 0.1 collective-permute-start.8
  50.0 14.0 %collective-permute-done.4.refs_1_ = f32[2,512,256]{2,1,0:T(8,128)S(1)} collective-permute-done((f32[2,512,256]{2,1,0:T(8,128)S(1)}, f32[2,512,256]{2,1,0:T(8,128)S(1)}, u32[]{:S(2)}, u32[]{:S(2)}) %collective-permute-start.4) | collective-permute-done | bytes 1048608 | tf_op jit(solution)/shard_map/ppermute | solution.py:359
  64.0 8.2 %collective-permute-start.9 = (f32[1,512,256]{2,1,0:T(8,128)S(1)}, f32[1,512,256]{2,1,0:T(8,128)S(1)}, u32[]{:S(2)}, u32[]{:S(2)}) collective-permute-start(f32[1,512,256]{2,1,0:T(8,128)S(1)} %get-tuple-element.58), channel_id=1, source_target_pairs={{4,8},{8,4},{12,16},{16,12},{20,24},{24,20},{28,32},{32,28},{36,40... | collective-permute-start | bytes 1572872 | tf_op jit(solution)/shard_map/ppermute | solution.py:359
  72.4 0.2 broadcast_in_dim.48.path
  72.6 0.0 copy-start
  72.6 6.7 %shard_map.60.cost.refs_5_ = f32[80,512,128]{2,1,0:T(8,128)S(1)} custom-call(f32[96,512]{1,0:T(8,128)S(1)} %bitcast.27), custom_call_target="tpu_custom_call" | custom-call | flops 1048576 | bytes 33554432 | tf_op jit(solution)/shard_map/pallas_call | solution.py:336
  79.3 20.6 %shard_map.61 = (f32[12,2,512,128]{3,2,1,0:T(8,128)S(1)}, f32[12,2,512,128]{3,2,1,0:T(8,128)S(1)}, f32[2,512,256]{2,1,0:T(8,128)S(1)}, f32[4,32,128]{2,1,0:T(8,128)S(1)}, f32[8,512,256]{2,1,0:T(8,128)}) custom-call(s32[2]{0:T(128)S(1)} %pad_add_fusion.info.refs_0_, f32[8,512,256]{2,1,0:T(8,128)} %own.3, f32[576,256]{1,0:T(8,128)} %collective-permute-done.lead1, ...), custom_call_target="tpu_custom_call" | custom-call | flops 1048576 | bytes 33554432 | tf_op jit(solution)/shard_map/pallas_call | solution.py:336
  99.9 5.9 %shard_map.62 = (f32[12,2,512,128]{3,2,1,0:T(8,128)S(1)}, f32[12,2,512,128]{3,2,1,0:T(8,128)S(1)}, f32[2,512,256]{2,1,0:T(8,128)S(1)}, f32[4,32,128]{2,1,0:T(8,128)S(1)}, f32[8,512,256]{2,1,0:T(8,128)}) custom-call(s32[2]{0:T(128)S(1)} %pad_add_fusion.info.refs_0_, ...), custom_call_target="tpu_custom_call", output_to_operand_aliasing={{0}: (6, {}), {1}: (7, {}), {4}: (10, {})} | custom-call | flops 1048576 | bytes 33554432 | tf_op jit(solution)/shard_map/pallas_call | solution.py:336
  105.9 5.9 %shard_map.63 = (f32[12,2,512,128]{3,2,1,0:T(8,128)S(1)}, f32[12,2,512,128]{3,2,1,0:T(8,128)S(1)}, f32[2,512,256]{2,1,0:T(8,128)S(1)}, f32[4,32,128]{2,1,0:T(8,128)S(1)}, f32[8,512,256]{2,1,0:T(8,128)}) custom-call(s32[2]{0:T(128)S(1)} %pad_add_fusion.info.refs_0_, ...), custom_call_target="tpu_custom_call", output_to_operand_aliasing={{0}: (6, {}), {1}: (7, {}), {4}: (10, {})} | custom-call | flops 1048576 | bytes 33554432 | tf_op jit(solution)/shard_map/pallas_call | solution.py:336
  111.8 6.2 %shard_map.64 = (f32[2,2,512,128]{3,2,1,0:T(8,128)S(1)}, f32[2,512,256]{2,1,0:T(8,128)S(1)}, f32[4,32,128]{2,1,0:T(8,128)S(1)}, f32[8,512,256]{2,1,0:T(8,128)}) custom-call(s32[2]{0:T(128)S(1)} %pad_add_fusion.info.refs_0_, f32[1,512,256]{2,1,0:T(8,128)S(1)} %collective-permute-done.2.refs_1_, ...), custom_call_target="tpu_custom_call", output_to_operand_aliasing={{3}: (10, {})} | custom-call | flops 1048576 | bytes 33554432 | tf_op jit(solution)/shard_map/pallas_call | solution.py:336
  118.0 1.4 %shard_map.65 = f32[4,32,128]{2,1,0:T(8,128)S(1)} custom-call(s32[2]{0:T(128)S(1)} %pad_add_fusion.info.refs_0_, f32[1,512,256]{2,1,0:T(8,128)S(1)} %collective-permute-done.8.got1, f32[1,512,256]{2,1,0:T(8,128)S(1)} %collective-permute-done.9.got2, s32[1,256]{1,0:T(1,128)S(1)} %bitcast.34, f32[1,256]{1,0:T(1,128)S(1)} %bitcast.39, ...), custom_call_target="tpu_custom_call" | custom-call | flops 1048576 | bytes 33554432 | tf_op jit(solution)/shard_map/pallas_call | solution.py:336
  119.4 0.1 collective-permute-start.10
  119.5 1.2 collective-permute-done.10
  120.7 1.1 collective-permute-start.11
  121.7 2.7 %collective-permute-done.11 = f32[1,32,128]{2,1,0:T(8,128)S(1)} collective-permute-done((f32[1,32,128]{2,1,0:T(8,128)S(1)}, f32[1,32,128]{2,1,0:T(8,128)S(1)}, u32[]{:S(2)}, u32[]{:S(2)}) %collective-permute-start.11) | collective-permute-done | bytes 16416 | tf_op jit(solution)/shard_map/ppermute | solution.py:453
  124.5 0.6 bitcast_multiply_fusion
  (30 shorter events, 0.2 us)
Async XLA Ops:
  0.6 19.1 %copy-start.2 = (f32[4,8,512]{2,1,0:T(8,128)S(1)}, f32[4,8,512]{2,1,0:T(8,128)}, u32[]{:S(2)}) copy-start(f32[4,8,512]{2,1,0:T(8,128)} %param.5) | copy-start | bytes 196612
  2.6 18.9 %collective-permute-start = (f32[576,256]{1,0:T(8,128)S(1)}, f32[576,256]{1,0:T(8,128)}, u32[]{:S(2)}, u32[]{:S(2)}) collective-permute-start(f32[576,256]{1,0:T(8,128)S(1)} %get-tuple-element.30), channel_id=1, source_target_pairs={{0,4},{4,0},{8,12},{12,8},{16,20},{20,16},{24,28},{28,24},{32,36},... | collective-permute-start | bytes 1769480 | tf_op jit(solution)/shard_map/ppermute | solution.py:359
  4.2 24.3 %collective-permute-start.1 = (f32[576,256]{1,0:T(8,128)S(1)}, f32[576,256]{1,0:T(8,128)}, u32[]{:S(2)}, u32[]{:S(2)}) collective-permute-start(f32[576,256]{1,0:T(8,128)S(1)} %get-tuple-element.31), channel_id=1, source_target_pairs={{4,8},{8,4},{12,16},{16,12},{20,24},{24,20},{28,32},{32,28},{36,40... | collective-permute-start | bytes 1769480 | tf_op jit(solution)/shard_map/ppermute | solution.py:359
  15.3 26.3 %collective-permute-start.6 = (f32[2,512,256]{2,1,0:T(8,128)}, f32[2,512,256]{2,1,0:T(8,128)}, u32[]{:S(2)}, u32[]{:S(2)}) collective-permute-start(f32[2,512,256]{2,1,0:T(8,128)} %get-tuple-element.63), channel_id=1, source_target_pairs={{0,4},{4,0},{8,12},{12,8},{16,20},{20,16},{24,28},{28,24},{32,36},... | collective-permute-start | bytes 3145736 | tf_op jit(solution)/shard_map/ppermute | solution.py:359
  15.3 34.6 %collective-permute-start.7 = (f32[2,512,256]{2,1,0:T(8,128)}, f32[2,512,256]{2,1,0:T(8,128)}, u32[]{:S(2)}, u32[]{:S(2)}) collective-permute-start(f32[2,512,256]{2,1,0:T(8,128)} %get-tuple-element.62), channel_id=1, source_target_pairs={{4,8},{8,4},{12,16},{16,12},{20,24},{24,20},{28,32},{32,28},{36,40... | collective-permute-start | bytes 3145736 | tf_op jit(solution)/shard_map/ppermute | solution.py:359
  18.5 45.5 %collective-permute-start.4 = (f32[2,512,256]{2,1,0:T(8,128)S(1)}, f32[2,512,256]{2,1,0:T(8,128)S(1)}, u32[]{:S(2)}, u32[]{:S(2)}) collective-permute-start(f32[2,512,256]{2,1,0:T(8,128)S(1)} %get-tuple-element.64), channel_id=1, source_target_pairs={{0,4},{4,0},{8,12},{12,8},{16,20},{20,16},{24,28},{28,24},{32,36},... | collective-permute-start | bytes 3145736 | tf_op jit(solution)/shard_map/ppermute | solution.py:359
  21.5 78.4 %collective-permute-start.5 = (f32[2,512,256]{2,1,0:T(8,128)S(1)}, f32[2,512,256]{2,1,0:T(8,128)S(1)}, u32[]{:S(2)}, u32[]{:S(2)}) collective-permute-start(f32[2,512,256]{2,1,0:T(8,128)S(1)} %get-tuple-element.64), channel_id=1, source_target_pairs={{4,8},{8,4},{12,16},{16,12},{20,24},{24,20},{28,32},{32,28},{36,40... | collective-permute-start | bytes 3145736 | tf_op jit(solution)/shard_map/ppermute | solution.py:359
  28.5 83.2 %collective-permute-start.2 = (f32[1,512,256]{2,1,0:T(8,128)S(1)}, f32[1,512,256]{2,1,0:T(8,128)S(1)}, u32[]{:S(2)}, u32[]{:S(2)}) collective-permute-start(f32[1,512,256]{2,1,0:T(8,128)S(1)} %get-tuple-element.61), channel_id=1, source_target_pairs={{0,4},{4,0},{8,12},{12,8},{16,20},{20,16},{24,28},{28,24},{32,36},... | collective-permute-start | bytes 1572872 | tf_op jit(solution)/shard_map/ppermute | solution.py:359
  41.7 70.1 %collective-permute-start.3 = (f32[1,512,256]{2,1,0:T(8,128)S(1)}, f32[1,512,256]{2,1,0:T(8,128)S(1)}, u32[]{:S(2)}, u32[]{:S(2)}) collective-permute-start(f32[1,512,256]{2,1,0:T(8,128)S(1)} %get-tuple-element.60), channel_id=1, source_target_pairs={{4,8},{8,4},{12,16},{16,12},{20,24},{24,20},{28,32},{32,28},{36,40... | collective-permute-start | bytes 1572872 | tf_op jit(solution)/shard_map/ppermute | solution.py:359
  49.9 68.0 %collective-permute-start.8 = (f32[1,512,256]{2,1,0:T(8,128)S(1)}, f32[1,512,256]{2,1,0:T(8,128)S(1)}, u32[]{:S(2)}, u32[]{:S(2)}) collective-permute-start(f32[1,512,256]{2,1,0:T(8,128)S(1)} %get-tuple-element.59), channel_id=1, source_target_pairs={{0,4},{4,0},{8,12},{12,8},{16,20},{20,16},{24,28},{28,24},{32,36},... | collective-permute-start | bytes 1572872 | tf_op jit(solution)/shard_map/ppermute | solution.py:359
  64.0 53.9 %collective-permute-start.9 = (f32[1,512,256]{2,1,0:T(8,128)S(1)}, f32[1,512,256]{2,1,0:T(8,128)S(1)}, u32[]{:S(2)}, u32[]{:S(2)}) collective-permute-start(f32[1,512,256]{2,1,0:T(8,128)S(1)} %get-tuple-element.58), channel_id=1, source_target_pairs={{4,8},{8,4},{12,16},{16,12},{20,24},{24,20},{28,32},{32,28},{36,40... | collective-permute-start | bytes 1572872 | tf_op jit(solution)/shard_map/ppermute | solution.py:359
  72.6 6.7 %copy-start = (s32[256]{0:T(256)S(1)}, s32[256]{0:T(256)}, u32[]{:S(2)}) copy-start(s32[256]{0:T(256)} %param.6) | copy-start | bytes 3076
  72.6 6.7 %copy-start.1 = (f32[256]{0:T(256)S(1)}, f32[256]{0:T(256)}, u32[]{:S(2)}) copy-start(f32[256]{0:T(256)} %param.7) | copy-start | bytes 3076
  119.4 1.3 %collective-permute-start.10 = (f32[2,32,128]{2,1,0:T(8,128)S(1)}, f32[2,32,128]{2,1,0:T(8,128)S(1)}, u32[]{:S(2)}, u32[]{:S(2)}) collective-permute-start(f32[2,32,128]{2,1,0:T(8,128)S(1)} %dynamic-slice_bitcast_fusion), channel_id=1, source_target_pairs={{0,1},{1,0},{2,3},{3,2},{4,5},{5,4},{6,7},{7,6},{8,9},{9,8},{10,11... | collective-permute-start | bytes 98312 | tf_op jit(solution)/shard_map/ppermute | solution.py:453
  120.7 3.8 %collective-permute-start.11 = (f32[1,32,128]{2,1,0:T(8,128)S(1)}, f32[1,32,128]{2,1,0:T(8,128)S(1)}, u32[]{:S(2)}, u32[]{:S(2)}) collective-permute-start(f32[1,32,128]{2,1,0:T(8,128)S(1)} %constant_dynamic-slice_fusion), channel_id=1, source_target_pairs={{0,2},{1,3},{2,0},{3,1},{4,6},{5,7},{6,4},{7,5},{8,10},{9,11},{10,... | collective-permute-start | bytes 49160 | tf_op jit(solution)/shard_map/ppermute | solution.py:453
